TPU v7x, 512 devices: a whole 4x8x8 slice. The times are simulated.
512 devices in a mesh: ctx: 128 (over y, z, core), head: 4 (over x).
Axes of the slice: x: 4, y: 8, z: 8, core: 2. Of those that a mesh axis runs over, the one named last changes fastest.
Arguments:
- tokens: bfloat16 [2, 16384, 4096], P(None, 'ctx', 'head'), may hold values from -6 to 6
- w_query: bfloat16 [4096, 2048], P('ctx', 'head'), may hold values from -0.09375 to 0.09375
- w_key: bfloat16 [4096, 2048], P('ctx', 'head'), may hold values from -0.09375 to 0.09375
- w_value: bfloat16 [4096, 2048], P('ctx', 'head'), may hold values from -0.09375 to 0.09375
- norm_gain: float32 [2048], P('head'), may hold values from 0.1 to 1.9
Outputs:
- attended: bfloat16 [2, 16384, 2048], P(None, 'ctx', 'head')
All inputs are finite; a program needn't handle non-finite values.
Results may differ from a plain program's by a relative error of at most 0.0072.
Values may be sent and summed in bfloat16 or wider, within the bound.
No kernel may reach another device: no remote copies, remote signals or barrier semaphores. Data moves between devices by JAX's collectives and lax.ppermute only.
A program may use at most 192 MiB of HBM per device.

v0:
```python
import jax
import jax.numpy as jnp
from jax import lax
from jax.sharding import PartitionSpec as P

HD = 128


def entering(part, axis, combine, identity):
    place = lax.axis_index(axis)
    gathered = lax.all_gather(part, axis)
    state = jnp.zeros_like(part) + jnp.asarray(identity, part.dtype)

    def one(hop, state):
        return combine(state, lax.dynamic_index_in_dim(gathered, hop, 0, False))

    return lax.fori_loop(0, place, one, state)


def add_states(earlier, later):
    return earlier + later


def body(tokens, w_query, w_key, w_value, norm_gain):
    gathered = lax.all_gather(tokens, "head", axis=2, tiled=True)
    seq_count, span_len, model_dim = gathered.shape
    token_rows = gathered.reshape(seq_count * span_len, model_dim)
    features = w_query.shape[1]
    query_full = lax.all_gather(w_query, "ctx", axis=0, tiled=True)
    query_sum = jnp.dot(token_rows, query_full, preferred_element_type=jnp.float32)
    key_full = lax.all_gather(w_key, "ctx", axis=0, tiled=True)
    key_sum = jnp.dot(token_rows, key_full, preferred_element_type=jnp.float32)
    value_full = lax.all_gather(w_value, "ctx", axis=0, tiled=True)
    value_sum = jnp.dot(token_rows, value_full, preferred_element_type=jnp.float32)
    head_count = features // HD

    def heads_first(projected):
        shaped = projected.astype(jnp.bfloat16).reshape(seq_count, span_len, head_count, HD)
        return shaped.transpose(0, 2, 1, 3)

    query = heads_first(jax.nn.silu(query_sum))
    key_all = heads_first(jax.nn.silu(key_sum))
    value_all = heads_first(value_sum)
    positions = jnp.arange(span_len)
    causal = positions[:, None] >= positions[None, :]
    scores = jnp.einsum("shtd,shud->shtu", query, key_all, preferred_element_type=jnp.float32)
    masked = jnp.where(causal, scores, 0.0).astype(jnp.bfloat16)
    local_out = jnp.einsum("shtu,shud->shtd", masked, value_all, preferred_element_type=jnp.float32)
    states = jnp.einsum("shud,shue->shde", key_all, value_all, preferred_element_type=jnp.float32)
    prefix = entering(states, "ctx", add_states, jnp.zeros_like(states))
    from_prefix = jnp.einsum(
        "shtd,shde->shte", query, prefix.astype(jnp.bfloat16), preferred_element_type=jnp.float32
    )
    total = local_out + from_prefix
    scale_inv = lax.rsqrt(jnp.mean(total * total, axis=-1, keepdims=True) + 1e-06)
    gain_view = norm_gain.reshape(1, head_count, 1, HD)
    normed = total * scale_inv * gain_view
    return normed.transpose(0, 2, 1, 3).reshape(seq_count, span_len, features).astype(jnp.bfloat16)


def solution(mesh):
    in_specs = (
        P(None, "ctx", "head"),
        P("ctx", "head"),
        P("ctx", "head"),
        P("ctx", "head"),
        P("head"),
    )
    out_specs = P(None, "ctx", "head")
    return jax.shard_map(body, mesh=mesh, in_specs=in_specs, out_specs=out_specs, check_vma=False)
```

profile of v0, /device:TPU:505, one launch (start us, length us, event | category | flops | bytes accessed | tf_op | source)
XLA Modules:
  0.0 681.2 jit_solution(4002791682843718653)
XLA Ops:
  9.4 35.0 %all-gather.7.cloned.1.call-done = bf16[2,128,4096]{2,1,0:T(8,128)(2,1)} async-done(((bf16[2,128,1024]{2,1,0:T(8,128)(2,1)}), bf16[2,128,4096]{2,1,0:T(8,128)(2,1)}) %all-gather.7.cloned.1.call-update) | async-done | bytes 2097168 | tf_op jit(solution)/shard_map/all_gather | solution.py:25
  44.3 84.9 %all-gather.11.cloned.1.call-done = bf16[4096,512]{1,0:T(8,128)(2,1)} async-done(((bf16[32,512]{1,0:T(8,128)(2,1)}), bf16[4096,512]{1,0:T(8,128)(2,1)}) %all-gather.11.cloned.1.call-update) | async-done | bytes 4194320 | tf_op jit(solution)/shard_map/all_gather | solution.py:31
  129.2 4.3 multiply_convert_fusion
  133.8 79.8 %all-gather.13.cloned.1.call-done = bf16[4096,512]{1,0:T(8,128)(2,1)} async-done(((bf16[32,512]{1,0:T(8,128)(2,1)}), bf16[4096,512]{1,0:T(8,128)(2,1)}) %all-gather.13.cloned.1.call-update) | async-done | bytes 4194320 | tf_op jit(solution)/shard_map/all_gather | solution.py:33
  213.6 3.4 convolution_convert_fusion
  218.2 79.6 %all-gather.9.cloned.1.call-done = bf16[4096,512]{1,0:T(8,128)(2,1)} async-done(((bf16[32,512]{1,0:T(8,128)(2,1)}), bf16[4096,512]{1,0:T(8,128)(2,1)}) %all-gather.9.cloned.1.call-update) | async-done | bytes 4194320 | tf_op jit(solution)/shard_map/all_gather | solution.py:29
  297.8 3.5 multiply_convert_fusion.1
  301.9 219.8 %all-gather.15.cloned.1.call-done = f32[256,4,128,128]{3,2,1,0:T(8,128)} async-done(((f32[2,4,128,128]{3,2,1,0:T(8,128)}), f32[256,4,128,128]{3,2,1,0:T(8,128)}) %all-gather.15.cloned.1.call-update) | async-done | bytes 67108880 | tf_op jit(solution)/shard_map/all_gather | solution.py:11
  521.7 151.5 %while.10 = (s32[]{:T(128)}, f32[2,4,128,128]{3,2,1,0:T(8,128)S(1)}, s32[]{:T(128)}, f32[128,2,4,128,128]{4,3,2,1,0:T(8,128)}, s32[]{:T(128)}, /*index=5*/s32[]{:T(128)}, s32[]{:T(128)}) while((s32[]{:T(128)}, f32[2,4,128,128]{3,2,1,0:T(8,128)S(1)}, s32[]{:T(128)}, f32[128,2,4,128,128]{4,3,2,1,0:T(8,128)}, s32[]{:T(128)}, ...), condition=%wide.region_1.2_spmd, body=%wide.region_0.1_spmd.sunk | while | flops 131077 | bytes 1572987 | solution.py:17
  525.3 1.2 bitcast_add_fusion.2
  526.5 1.2 bitcast_add_fusion.2
  527.7 1.2 bitcast_add_fusion.2
  528.9 1.2 bitcast_add_fusion.2
  530.1 1.2 bitcast_add_fusion.2
  531.3 1.2 bitcast_add_fusion.2
  536.1 1.2 bitcast_add_fusion.2
  537.3 1.2 bitcast_add_fusion.2
  538.4 1.2 bitcast_add_fusion.2
  539.6 1.2 bitcast_add_fusion.2
  540.8 1.2 bitcast_add_fusion.2
  542.0 1.2 bitcast_add_fusion.2
  548.0 1.2 bitcast_add_fusion.2
  549.2 1.2 bitcast_add_fusion.2
  550.4 1.2 bitcast_add_fusion.2
  551.6 1.2 bitcast_add_fusion.2
  552.8 1.2 bitcast_add_fusion.2
  554.0 1.2 bitcast_add_fusion.2
  558.7 1.2 bitcast_add_fusion.2
  559.9 1.2 bitcast_add_fusion.2
  561.1 1.2 bitcast_add_fusion.2
  562.3 1.2 bitcast_add_fusion.2
  563.5 1.2 bitcast_add_fusion.2
  564.7 1.2 bitcast_add_fusion.2
  570.7 1.2 bitcast_add_fusion.2
  571.9 1.2 bitcast_add_fusion.2
  573.1 1.2 bitcast_add_fusion.2
  574.2 1.2 bitcast_add_fusion.2
  575.4 1.2 bitcast_add_fusion.2
  576.6 1.2 bitcast_add_fusion.2
  581.4 1.2 bitcast_add_fusion.2
  582.6 1.2 bitcast_add_fusion.2
  583.8 1.2 bitcast_add_fusion.2
  585.0 1.2 bitcast_add_fusion.2
  586.2 1.2 bitcast_add_fusion.2
  587.4 1.2 bitcast_add_fusion.2
  593.3 1.2 bitcast_add_fusion.2
  594.5 1.2 bitcast_add_fusion.2
  595.7 1.2 bitcast_add_fusion.2
  596.9 1.2 bitcast_add_fusion.2
  598.1 1.2 bitcast_add_fusion.2
  599.3 1.2 bitcast_add_fusion.2
  604.1 1.2 bitcast_add_fusion.2
  605.3 1.2 bitcast_add_fusion.2
  606.5 1.2 bitcast_add_fusion.2
  607.7 1.2 bitcast_add_fusion.2
  608.8 1.2 bitcast_add_fusion.2
  610.0 1.2 bitcast_add_fusion.2
  616.0 1.2 bitcast_add_fusion.2
  617.2 1.2 bitcast_add_fusion.2
  618.4 1.2 bitcast_add_fusion.2
  619.6 1.2 bitcast_add_fusion.2
  620.8 1.2 bitcast_add_fusion.2
  622.0 1.2 bitcast_add_fusion.2
  626.7 1.2 bitcast_add_fusion.2
  (98 shorter events, 90.4 us)
Async XLA Ops:
  6.5 37.8 %all-gather.7.cloned.1.call-start = ((), (), s32[]{:S(2)}) async-start(), calls=%async_computation | async-start | bytes 2621440 | tf_op jit(solution)/shard_map/all_gather | solution.py:25
  7.3 122.0 %all-gather.11.cloned.1.call-start = ((), (), s32[]{:S(2)}) async-start(), calls=%async_computation.2 | async-start | bytes 4227072 | tf_op jit(solution)/shard_map/all_gather | solution.py:31
  8.0 205.6 %all-gather.13.cloned.1.call-start = ((), (), s32[]{:S(2)}) async-start(), calls=%async_computation.3 | async-start | bytes 4227072 | tf_op jit(solution)/shard_map/all_gather | solution.py:33
  8.7 289.1 %all-gather.9.cloned.1.call-start = ((), (), s32[]{:S(2)}) async-start(), calls=%async_computation.1 | async-start | bytes 4227072 | tf_op jit(solution)/shard_map/all_gather | solution.py:29
  9.3 512.4 %all-gather.15.cloned.1.call-start = ((), (), s32[]{:S(2)}) async-start(), calls=%async_computation.4 | async-start | bytes 67633152 | tf_op jit(solution)/shard_map/all_gather | solution.py:11
  129.2 84.4 %copy-start.1 = (bf16[2,128,4096]{2,1,0:T(8,128)(2,1)S(1)}, bf16[2,128,4096]{2,1,0:T(8,128)(2,1)}, u32[]{:S(2)}) copy-start(bf16[2,128,4096]{2,1,0:T(8,128)(2,1)} %all-gather.7.cloned.1.call-done) | copy-start | bytes 6291460
  521.7 151.9 %copy-start = (f32[512]{0:T(512)S(1)}, f32[512]{0:T(512)}, u32[]{:S(2)}) copy-start(f32[512]{0:T(512)} %param.11) | copy-start | bytes 6148
Sparse Core Ops, SparseCore 0:
  9.4 34.8 all-gather.6
  47.5 81.7 all-gather.10
  132.4 81.1 all-gather.12
  216.6 81.1 all-gather.8
  300.8 220.8 all-gather.14
where the time goes:
time: 687 us; the launch traced here: 681 us
  waiting for transfers between devices  502 us (73%)
  other arithmetic  149 us (22%)
  between operations  13.2 us (2%)
  matrix products  13.1 us (2%)
    all_gather x1, waiting for transfers between devices, entering(): gathered = lax.all_gather(part, axis)  220 us
    add x127, other arithmetic, add_states(): return earlier + later  149 us
    all_gather x1, waiting for transfers between devices, body(): key_full = lax.all_gather(w_key, 'ctx', axis=0, tiled=True)  84.9 us
    all_gather x1, waiting for transfers between devices, body(): value_full = lax.all_gather(w_value, 'ctx', axis=0, tiled=True)  79.8 us
    all_gather x1, waiting for transfers between devices, body(): query_full = lax.all_gather(w_query, 'ctx', axis=0, tiled=True)  79.6 us
    all_gather x1, waiting for transfers between devices, body(): gathered = lax.all_gather(tokens, 'head', axis=2, tiled=True)  35 us
  transfers between devices with their start and end apart: 5, of which 5 were waited for; matrix products, arithmetic and copies ran while one was open for 2% of the time, Pallas kernels for 0%

commit v1 on v0

--- a/solution.py
+++ b/solution.py
@@ -22,7 +22,9 @@
 
 
 def body(tokens, w_query, w_key, w_value, norm_gain):
-    gathered = lax.all_gather(tokens, "head", axis=2, tiled=True)
+    gathered = jnp.concatenate(
+        lax.all_to_all(jnp.stack([tokens] * lax.axis_size("head")), "head", 0, 0), axis=2
+    )
     seq_count, span_len, model_dim = gathered.shape
     token_rows = gathered.reshape(seq_count * span_len, model_dim)
     features = w_query.shape[1]

time: 687 us -> 649 us (0.945)
  waiting for transfers between devices: 502 us -> 431 us
  blocking collectives: 0 us -> 29.3 us
    all_gather x1 -> x0, waiting for transfers between devices: 35 us -> none  [body(): gathered = lax.all_gather(tokens, 'head', axis=2, tiled=True)]
    all_gather x1, waiting for transfers between devices: 79.8 us -> 49 us  [body(): value_full = lax.all_gather(w_value, 'ctx', axis=0, tiled=True)]
    all_to_all x0 -> x1, blocking collectives: none -> 29.3 us  [body(): lax.all_to_all(jnp.stack([tokens] * lax.axis_size('head')), 'head', 0, 0)]
  transfers between devices with their start and end apart: 5 -> 4, of which waited for: 5 -> 4; matrix products, arithmetic and copies ran while one was open for 2% -> 3% of each run, Pallas kernels for 0% -> 0%
where the time goes in v1:
time: 649 us; the launch traced here: 643 us
  waiting for transfers between devices  431 us (66%)
  other arithmetic  149 us (23%)
  blocking collectives  29.3 us (5%)
  between operations  13.2 us (2%)
  matrix products  12.3 us (2%)
    all_gather x1, waiting for transfers between devices, entering(): gathered = lax.all_gather(part, axis)  220 us
    add x127, other arithmetic, add_states(): return earlier + later  149 us
    all_gather x1, waiting for transfers between devices, body(): key_full = lax.all_gather(w_key, 'ctx', axis=0, tiled=True)  80.9 us
    all_gather x1, waiting for transfers between devices, body(): query_full = lax.all_gather(w_query, 'ctx', axis=0, tiled=True)  79.5 us
    all_gather x1, waiting for transfers between devices, body(): value_full = lax.all_gather(w_value, 'ctx', axis=0, tiled=True)  49 us
    all_to_all x1, blocking collectives, body(): lax.all_to_all(jnp.stack([tokens] * lax.axis_size('head')), 'head', 0, 0)  29.3 us
  transfers between devices with their start and end apart: 4, of which 4 were waited for; matrix products, arithmetic and copies ran while one was open for 3% of the time, Pallas kernels for 0%

profile of v1, /device:TPU:505, one launch (start us, length us, event | category | flops | bytes accessed | tf_op | source)
XLA Modules:
  0.0 643.0 jit_solution(12263145506521153286)
XLA Ops:
  8.8 1.3 stack.2
  10.1 29.3 %all_to_all.5 = bf16[4,2,128,1024]{3,2,1,0:T(8,128)(2,1)S(1)} all-to-all(bf16[4,2,128,1024]{3,2,1,0:T(8,128)(2,1)S(1)} %stack.2), channel_id=1, replica_groups=mesh['ctx'=128,'head'=4] {'head'}, dimensions={0} | all-to-all | bytes 4194304 | tf_op jit(solution)/shard_map/all_to_all | solution.py:26
  39.4 1.6 copy.18
  41.9 49.0 %all-gather.10.cloned.1.call-done = bf16[4096,512]{1,0:T(8,128)(2,1)} async-done(((bf16[32,512]{1,0:T(8,128)(2,1)}), bf16[4096,512]{1,0:T(8,128)(2,1)}) %all-gather.10.cloned.1.call-update) | async-done | bytes 4194320 | tf_op jit(solution)/shard_map/all_gather | solution.py:35
  90.9 3.4 convolution_convert_fusion
  94.4 80.9 %all-gather.8.cloned.1.call-done = bf16[4096,512]{1,0:T(8,128)(2,1)} async-done(((bf16[32,512]{1,0:T(8,128)(2,1)}), bf16[4096,512]{1,0:T(8,128)(2,1)}) %all-gather.8.cloned.1.call-update) | async-done | bytes 4194320 | tf_op jit(solution)/shard_map/all_gather | solution.py:33
  175.3 3.5 multiply_convert_fusion
  180.2 79.5 %all-gather.6.cloned.1.call-done = bf16[4096,512]{1,0:T(8,128)(2,1)} async-done(((bf16[32,512]{1,0:T(8,128)(2,1)}), bf16[4096,512]{1,0:T(8,128)(2,1)}) %all-gather.6.cloned.1.call-update) | async-done | bytes 4194320 | tf_op jit(solution)/shard_map/all_gather | solution.py:31
  259.7 3.5 multiply_convert_fusion.1
  263.7 219.8 %all-gather.12.cloned.1.call-done = f32[256,4,128,128]{3,2,1,0:T(8,128)} async-done(((f32[2,4,128,128]{3,2,1,0:T(8,128)}), f32[256,4,128,128]{3,2,1,0:T(8,128)}) %all-gather.12.cloned.1.call-update) | async-done | bytes 67108880 | tf_op jit(solution)/shard_map/all_gather | solution.py:11
  483.6 151.5 %while.10 = (s32[]{:T(128)}, f32[2,4,128,128]{3,2,1,0:T(8,128)S(1)}, s32[]{:T(128)}, f32[128,2,4,128,128]{4,3,2,1,0:T(8,128)}, s32[]{:T(128)}, /*index=5*/s32[]{:T(128)}, s32[]{:T(128)}) while((s32[]{:T(128)}, f32[2,4,128,128]{3,2,1,0:T(8,128)S(1)}, s32[]{:T(128)}, f32[128,2,4,128,128]{4,3,2,1,0:T(8,128)}, s32[]{:T(128)}, ...), condition=%wide.region_1.2_spmd, body=%wide.region_0.1_spmd.sunk | while | flops 131077 | bytes 1572987 | solution.py:17
  483.6 1.2 bitcast_add_fusion.2
  484.8 1.2 bitcast_add_fusion.2
  486.0 1.2 bitcast_add_fusion.2
  487.2 1.2 bitcast_add_fusion.2
  491.9 1.2 bitcast_add_fusion.2
  493.1 1.2 bitcast_add_fusion.2
  494.3 1.2 bitcast_add_fusion.2
  495.5 1.2 bitcast_add_fusion.2
  496.7 1.2 bitcast_add_fusion.2
  497.9 1.2 bitcast_add_fusion.2
  503.9 1.2 bitcast_add_fusion.2
  505.1 1.2 bitcast_add_fusion.2
  506.3 1.2 bitcast_add_fusion.2
  507.5 1.2 bitcast_add_fusion.2
  508.6 1.2 bitcast_add_fusion.2
  509.8 1.2 bitcast_add_fusion.2
  514.6 1.2 bitcast_add_fusion.2
  515.8 1.2 bitcast_add_fusion.2
  517.0 1.2 bitcast_add_fusion.2
  518.2 1.2 bitcast_add_fusion.2
  519.4 1.2 bitcast_add_fusion.2
  520.6 1.2 bitcast_add_fusion.2
  526.5 1.2 bitcast_add_fusion.2
  527.7 1.2 bitcast_add_fusion.2
  528.9 1.2 bitcast_add_fusion.2
  530.1 1.2 bitcast_add_fusion.2
  531.3 1.2 bitcast_add_fusion.2
  532.5 1.2 bitcast_add_fusion.2
  537.3 1.2 bitcast_add_fusion.2
  538.5 1.2 bitcast_add_fusion.2
  539.7 1.2 bitcast_add_fusion.2
  540.9 1.2 bitcast_add_fusion.2
  542.1 1.2 bitcast_add_fusion.2
  543.2 1.2 bitcast_add_fusion.2
  549.2 1.2 bitcast_add_fusion.2
  550.4 1.2 bitcast_add_fusion.2
  551.6 1.2 bitcast_add_fusion.2
  552.8 1.2 bitcast_add_fusion.2
  554.0 1.2 bitcast_add_fusion.2
  555.2 1.2 bitcast_add_fusion.2
  560.0 1.2 bitcast_add_fusion.2
  561.1 1.2 bitcast_add_fusion.2
  562.3 1.2 bitcast_add_fusion.2
  563.5 1.2 bitcast_add_fusion.2
  564.7 1.2 bitcast_add_fusion.2
  565.9 1.2 bitcast_add_fusion.2
  571.9 1.2 bitcast_add_fusion.2
  573.1 1.2 bitcast_add_fusion.2
  574.3 1.2 bitcast_add_fusion.2
  575.5 1.2 bitcast_add_fusion.2
  576.7 1.2 bitcast_add_fusion.2
  577.9 1.2 bitcast_add_fusion.2
  582.6 1.2 bitcast_add_fusion.2
  (97 shorter events, 93.0 us)
Async XLA Ops:
  6.5 84.4 %all-gather.10.cloned.1.call-start = ((), (), s32[]{:S(2)}) async-start(), calls=%async_computation.3 | async-start | bytes 4227072 | tf_op jit(solution)/shard_map/all_gather | solution.py:35
  7.3 168.0 %all-gather.8.cloned.1.call-start = ((), (), s32[]{:S(2)}) async-start(), calls=%async_computation.2 | async-start | bytes 4227072 | tf_op jit(solution)/shard_map/all_gather | solution.py:33
  8.0 251.7 %all-gather.6.cloned.1.call-start = ((), (), s32[]{:S(2)}) async-start(), calls=%async_computation.1 | async-start | bytes 4227072 | tf_op jit(solution)/shard_map/all_gather | solution.py:31
  8.7 474.8 %all-gather.12.cloned.1.call-start = ((), (), s32[]{:S(2)}) async-start(), calls=%async_computation.4 | async-start | bytes 67633152 | tf_op jit(solution)/shard_map/all_gather | solution.py:11
  483.6 151.9 %copy-start = (f32[512]{0:T(512)S(1)}, f32[512]{0:T(512)}, u32[]{:S(2)}) copy-start(f32[512]{0:T(512)} %param.11) | copy-start | bytes 6148
Sparse Core Ops, SparseCore 0:
  10.5 80.4 all-gather.9
  94.1 81.1 all-gather.7
  178.4 81.1 all-gather.5
  262.6 220.8 all-gather.11
